TPU v7x, 256 devices: a whole 4x4x8 slice. The times are simulated.
256 devices in a mesh: seq: 16 (over x_lo, z), tp: 16 (over x_hi, y, core).
Axes of the slice: x: 4 (x_hi: 2, x_lo: 2; x = x_hi * 2 + x_lo), y: 4, z: 8, core: 2. Of those that a mesh axis runs over, the one named last changes fastest.
Arguments:
- tokens: bfloat16 [8192, 2048], P('seq', 'tp'), may hold values from -6 to 6
- w_first: bfloat16 [16, 512, 512], P('seq'), may hold values from -0.25 to 0.25
- second_factor_weight: bfloat16 [512, 16, 16], P('seq'), may hold values from -1.5 to 1.5
- w_up: bfloat16 [64, 2, 128, 128], P('tp'), may hold values from -0.375 to 0.375
- w_self: bfloat16 [6, 64, 128, 128], P(None, 'tp'), may hold values from -0.375 to 0.375
- w_cross: bfloat16 [6, 64, 128, 128], P(None, 'tp'), may hold values from -0.375 to 0.375
- w_down: bfloat16 [64, 2, 128, 128], P('tp'), may hold values from -0.1875 to 0.1875
- block_pairs: int32 [64, 2], P('tp'), may hold values from 0 to 15, all different within a row
- cotangent: bfloat16 [8192, 2048], P('seq', 'tp'), may hold values from -6 to 6
Outputs:
- layer_out: bfloat16 [8192, 2048], P('seq', 'tp')
- grad_tokens: bfloat16 [8192, 2048], P('seq', 'tp')
- grad_first: float32 [16, 512, 512], P('seq')
- gradient_second_factor: float32 [512, 16, 16], P('seq')
- grad_self: float32 [6, 64, 128, 128], P(None, 'tp', 'seq')
- grad_cross: float32 [6, 64, 128, 128], P(None, 'tp', 'seq')
Inputs may be any that keep to these rules, and one draw needn't show every extreme that they name: `block_pairs`: each row names two different input blocks, and every one of the 16 input blocks is named by some row.
All inputs are finite; a program needn't handle non-finite values.
Results may differ from a plain program's by a relative error of at most 0.019.
Values may be sent and summed in bfloat16 or wider, within the bound.
No kernel may reach another device: no remote copies, remote signals or barrier semaphores. Data moves between devices by JAX's collectives and lax.ppermute only.
A program may use at most 64 MiB of HBM per device.

v0:
```python
import math
import jax
import jax.numpy as jnp
from jax import lax
from jax.sharding import PartitionSpec as P


def partner_2(value, axis, bit):
    mask = 2**bit
    pairs = [(source, source ^ mask) for source in range(lax.axis_size(axis))]
    return lax.ppermute(value, axis, pairs)


def gelu_tanh(value):
    return jax.nn.gelu(value, approximate=True)


def swap_local(state, level):
    span = 2**level
    shape = state.shape
    folded = state.reshape(shape[0], shape[1] // (2 * span), 2, span, shape[2])
    return jnp.flip(folded, axis=2).reshape(shape)


def apply_blocks(state, weight):
    return jnp.einsum("rjc,jce->rje", state, weight, preferred_element_type=jnp.float32)


def apply_transposed(state, weight):
    return jnp.einsum("rje,jce->rjc", state, weight, preferred_element_type=jnp.float32)


def outer_blocks(left, right):
    return jnp.einsum("rjc,rje->jce", left, right, preferred_element_type=jnp.float32)


def per_device(
    tokens, w_first, second_factor_weight, w_up, w_self, w_cross, w_down, block_pairs, cotangent
):
    seq_len, width_local = tokens.shape
    group_count, block_len, _ = w_first.shape
    levels = w_self.shape[0]
    slots = w_self.shape[1]
    block_width = w_self.shape[2]
    model_width = width_local * lax.axis_size("tp")
    in_blocks = model_width // block_width
    local_bits = slots.bit_length() - 1
    total_tokens = seq_len * lax.axis_size("seq")
    token_scale = 1.0 / math.sqrt(total_tokens)
    model_width_scale = 1.0 / math.sqrt(model_width)
    grouped = tokens.reshape(group_count, block_len, width_local)
    first_factor_output = jnp.einsum(
        "acb,abd->acd", w_first, grouped, preferred_element_type=jnp.float32
    ).astype(jnp.bfloat16)
    received_rows = lax.all_to_all(
        first_factor_output, "seq", split_axis=1, concat_axis=0, tiled=True
    )
    mixed_part = jnp.einsum(
        "vyi,ivz->yvz", second_factor_weight, received_rows, preferred_element_type=jnp.float32
    ).astype(jnp.bfloat16)
    returned = lax.all_to_all(mixed_part, "seq", split_axis=0, concat_axis=1, tiled=True)
    mixed_tokens = returned
    first_factor_shifted = received_rows
    hidden_in = (
        tokens.astype(jnp.float32) + mixed_tokens.reshape(seq_len, width_local).astype(jnp.float32)
    ).astype(jnp.bfloat16)
    hidden_all, cotangent_all = (
        lax.all_gather(hidden_in, "tp", axis=1, tiled=True),
        lax.all_gather(cotangent, "tp", axis=1, tiled=True),
    )
    flat_pairs = block_pairs.reshape(-1)
    chosen = (
        block_pairs[:, :, None] == jnp.arange(in_blocks, dtype=jnp.int32)[None, None, :]
    ).astype(jnp.float32)
    picked = jnp.take(
        hidden_all.reshape(seq_len, in_blocks, block_width), flat_pairs, axis=1
    ).reshape(seq_len, slots, 2, block_width)
    state = jnp.einsum("rjkc,jkce->rje", picked, w_up, preferred_element_type=jnp.float32).astype(
        jnp.bfloat16
    )
    states = [state]
    partners = [None] * levels
    for level_at in range(levels):
        if level_at < local_bits:
            partner = swap_local(state, level_at)
        else:
            partner = partner_2(state, "tp", level_at - local_bits)
        partners[level_at] = partner
        state = (
            apply_blocks(state, w_self[level_at]) + apply_blocks(partner, w_cross[level_at])
        ).astype(jnp.bfloat16)
        states.append(state)
    top = state.astype(jnp.float32)
    activated = gelu_tanh(top).astype(jnp.bfloat16)
    pieces = jnp.einsum("rjc,jkce->rjke", activated, w_down, preferred_element_type=jnp.float32)
    down_term = jnp.einsum(
        "rjke,jki->rie", pieces, chosen, precision=lax.Precision.HIGHEST
    ).reshape(seq_len, model_width)
    down_part = lax.psum_scatter(down_term, "tp", scatter_dimension=1, tiled=True)
    layer_out = (hidden_in.astype(jnp.float32) + down_part).astype(jnp.bfloat16)
    grad_picked = jnp.take(
        cotangent_all.reshape(seq_len, in_blocks, block_width), flat_pairs, axis=1
    ).reshape(seq_len, slots, 2, block_width)
    grad_act = jnp.einsum("rjke,jkce->rjc", grad_picked, w_down, preferred_element_type=jnp.float32)
    _, pull = jax.vjp(gelu_tanh, top)
    grad_state = pull(grad_act)[0].astype(jnp.bfloat16)
    self_terms = [None] * levels
    cross_terms = [None] * levels
    for level_at in reversed(range(levels)):
        below = states[level_at]
        self_terms[level_at] = outer_blocks(below, grad_state)
        swap_bit = level_at - local_bits
        if level_at < local_bits:
            cross_terms[level_at] = outer_blocks(partners[level_at], grad_state)
            incoming = swap_local(apply_transposed(grad_state, w_cross[level_at]), level_at)
        else:
            cross_terms[level_at] = outer_blocks(partners[level_at], grad_state)
            incoming = partner_2(apply_transposed(grad_state, w_cross[level_at]), "tp", swap_bit)
        grad_state = (apply_transposed(grad_state, w_self[level_at]) + incoming).astype(
            jnp.bfloat16
        )
    back_pieces = jnp.einsum("rje,jkce->rjkc", grad_state, w_up, preferred_element_type=jnp.float32)
    spread = jnp.einsum(
        "rjkc,jki->ric", back_pieces, chosen, precision=lax.Precision.HIGHEST
    ).reshape(seq_len, model_width)
    spread_part = lax.psum_scatter(spread, "tp", scatter_dimension=1, tiled=True)
    grad_hidden = (cotangent.astype(jnp.float32) + spread_part).astype(jnp.bfloat16)
    level_self, level_cross = (
        lax.psum_scatter(jnp.stack(self_terms), "seq", scatter_dimension=2, tiled=True),
        lax.psum_scatter(jnp.stack(cross_terms), "seq", scatter_dimension=2, tiled=True),
    )
    received_rows = lax.all_to_all(
        grad_hidden.reshape(group_count, block_len, width_local),
        "seq",
        split_axis=1,
        concat_axis=0,
        tiled=True,
    )
    moved_back = jnp.einsum(
        "emj,meg->jeg", second_factor_weight, received_rows, preferred_element_type=jnp.float32
    ).astype(jnp.bfloat16)
    returned = lax.all_to_all(moved_back, "seq", split_axis=0, concat_axis=1, tiled=True)
    second_part = jnp.einsum(
        "tfm,lfm->ftl", received_rows, first_factor_shifted, preferred_element_type=jnp.float32
    )
    first_part = jnp.einsum("acd,abd->acb", returned, grouped, preferred_element_type=jnp.float32)
    second_sum, first_sum = lax.psum((second_part, first_part), "tp")
    grad_mix = jnp.einsum(
        "acb,acd->abd", w_first, returned, preferred_element_type=jnp.float32
    ).reshape(seq_len, width_local)
    grad_tokens = (grad_hidden.astype(jnp.float32) + grad_mix).astype(jnp.bfloat16)
    return (
        layer_out,
        grad_tokens,
        first_sum * model_width_scale,
        second_sum * model_width_scale,
        level_self * token_scale,
        level_cross * token_scale,
    )


def solution(mesh):
    in_specs = (
        P("seq", "tp"),
        P("seq", None, None),
        P("seq", None, None),
        P("tp", None, None, None),
        P(None, "tp", None, None),
        P(None, "tp", None, None),
        P("tp", None, None, None),
        P("tp", None),
        P("seq", "tp"),
    )
    out_specs = (
        P("seq", "tp"),
        P("seq", "tp"),
        P("seq", None, None),
        P("seq", None, None),
        P(None, "tp", "seq", None),
        P(None, "tp", "seq", None),
    )
    return jax.shard_map(
        per_device, mesh=mesh, in_specs=in_specs, out_specs=out_specs, check_vma=False
    )
```

profile of v0, /device:TPU:1, one launch (start us, length us, event | category | flops | bytes accessed | tf_op | source)
XLA Modules:
  0.0 764.0 jit_solution(14847866580858052665)
XLA Ops:
  13.0 10.0 %all-to-all-start = ((bf16[16,2,2048]{2,1,0:T(2,128)(2,1)}), bf16[16,2,2048]{2,1,0:T(2,128)(2,1)S(1)}, u32[]{:S(2)}, u32[]{:S(2)}) async-start(bf16[16,2,2048]{2,1,0:T(2,128)(2,1)} %reshape.151), calls=%async_computation | async-start | bytes 262144 | tf_op jit(solution)/shard_map/all_to_all | solution.py:55
  23.3 7.3 all-to-all-done
  31.0 10.6 %all_to_all.42 = bf16[16,32,128]{2,1,0:T(8,128)(2,1)S(1)} all-to-all(bf16[16,32,128]{2,1,0:T(8,128)(2,1)S(1)} %copy.138), channel_id=1, replica_groups=mesh['seq'=16,'tp'=16] {'seq'}, dimensions={0} | all-to-all | bytes 262144 | tf_op jit(solution)/shard_map/all_to_all | solution.py:61
  42.6 25.5 %all-gather.5.cloned.1.call-done = bf16[512,2048]{0,1:T(8,128)(2,1)} async-done(((bf16[512,128]{0,1:T(8,128)(2,1)}), bf16[512,2048]{0,1:T(8,128)(2,1)}) %all-gather.5.cloned.1.call-update) | async-done | bytes 2097168 | tf_op jit(solution)/shard_map/all_gather | solution.py:69
  68.1 3.0 copy.149
  72.8 49.2 %all-gather.3.cloned.1.call-done = bf16[512,2048]{1,0:T(8,128)(2,1)} async-done(((bf16[512,128]{1,0:T(8,128)(2,1)}), bf16[512,2048]{1,0:T(8,128)(2,1)}) %all-gather.3.cloned.1.call-update) | async-done | bytes 2097168 | tf_op jit(solution)/shard_map/all_gather | solution.py:68
  122.0 2.9 copy.140
  124.9 2.4 copy.141
  127.3 2.4 gather_fusion
  139.7 12.8 %collective-permute-done.1 = bf16[512,4,128]{2,0,1:T(8,128)(2,1)S(1)} collective-permute-done((bf16[512,4,128]{2,0,1:T(8,128)(2,1)S(1)}, bf16[512,4,128]{2,0,1:T(8,128)(2,1)S(1)}, u32[]{:S(2)}, u32[]{:S(2)}) %collective-permute-start.1) | collective-permute-done | bytes 524320 | tf_op jit(solution)/shard_map/ppermute | solution.py:11
  154.4 12.5 %collective-permute-done.2 = bf16[512,4,128]{2,0,1:T(8,128)(2,1)S(1)} collective-permute-done((bf16[512,4,128]{2,0,1:T(8,128)(2,1)S(1)}, bf16[512,4,128]{2,0,1:T(8,128)(2,1)S(1)}, u32[]{:S(2)}, u32[]{:S(2)}) %collective-permute-start.2) | collective-permute-done | bytes 524320 | tf_op jit(solution)/shard_map/ppermute | solution.py:11
  167.8 12.5 %collective-permute-done.3 = bf16[512,4,128]{2,0,1:T(8,128)(2,1)S(1)} collective-permute-done((bf16[512,4,128]{2,0,1:T(8,128)(2,1)S(1)}, bf16[512,4,128]{2,0,1:T(8,128)(2,1)S(1)}, u32[]{:S(2)}, u32[]{:S(2)}) %collective-permute-start.3) | collective-permute-done | bytes 524320 | tf_op jit(solution)/shard_map/ppermute | solution.py:11
  182.2 23.2 %collective-permute-done.4 = f32[512,4,128]{2,0,1:T(8,128)S(1)} collective-permute-done((f32[512,4,128]{2,0,1:T(8,128)S(1)}, f32[512,4,128]{2,0,1:T(8,128)S(1)}, u32[]{:S(2)}, u32[]{:S(2)}) %collective-permute-start.4) | collective-permute-done | bytes 1048608 | tf_op jit(solution)/shard_map/ppermute | solution.py:11
  207.3 21.5 %collective-permute-done.5 = f32[512,4,128]{2,0,1:T(8,128)S(1)} collective-permute-done((f32[512,4,128]{2,0,1:T(8,128)S(1)}, f32[512,4,128]{2,0,1:T(8,128)S(1)}, u32[]{:S(2)}, u32[]{:S(2)}) %collective-permute-start.5) | collective-permute-done | bytes 1048608 | tf_op jit(solution)/shard_map/ppermute | solution.py:11
  230.1 19.1 %collective-permute-done.6 = f32[512,4,128]{2,0,1:T(8,128)S(1)} collective-permute-done((f32[512,4,128]{2,0,1:T(8,128)S(1)}, f32[512,4,128]{2,0,1:T(8,128)S(1)}, u32[]{:S(2)}, u32[]{:S(2)}) %collective-permute-start.6) | collective-permute-done | bytes 1048608 | tf_op jit(solution)/shard_map/ppermute | solution.py:11
  249.8 6.0 collective-permute-start.7
  255.8 2.3 collective-permute-done.7
  259.6 2.3 rev.18
  268.0 3.3 convolution_bitcast_fusion.1
  271.2 7.2 convolution_bitcast_fusion
  278.5 5.4 copy.192
  285.6 4.1 fusion.1
  289.7 4.0 copy.210
  309.2 59.9 %reduce-scatter.7.cloned.1.call-done = f32[512,128]{0,1:T(8,128)} async-done(((f32[512,2048]{0,1:T(8,128)}), f32[512,128]{0,1:T(8,128)}) %reduce-scatter.7.cloned.1.call-update) | async-done | bytes 262160 | tf_op jit(solution)/shard_map/reduce_scatter | solution.py:126
  371.8 14.1 %all_to_all.43 = bf16[16,2,2048]{2,1,0:T(2,128)(2,1)S(1)} all-to-all(bf16[16,2,2048]{2,1,0:T(2,128)(2,1)S(1)} %reshape.153), channel_id=1, replica_groups=mesh['seq'=16,'tp'=16] {'seq'}, dimensions={0} | all-to-all | bytes 262144 | tf_op jit(solution)/shard_map/all_to_all | solution.py:132
  386.9 3.5 all-to-all-start.3
  390.5 70.1 %reduce-scatter.5.cloned.1.call-done = f32[512,128]{1,0:T(8,128)} async-done(((f32[512,2048]{1,0:T(8,128)}), f32[512,128]{1,0:T(8,128)}) %reduce-scatter.5.cloned.1.call-update) | async-done | bytes 262160 | tf_op jit(solution)/shard_map/reduce_scatter | solution.py:99
  463.6 62.4 %reduce-scatter.11.cloned.1.call-done = f32[6,4,8,128]{3,2,1,0:T(8,128)} async-done(((f32[6,4,128,128]{3,2,1,0:T(8,128)}), f32[6,4,8,128]{3,2,1,0:T(8,128)}) %reduce-scatter.11.cloned.1.call-update) | async-done | bytes 98320 | tf_op jit(solution)/shard_map/reduce_scatter | solution.py:130
  527.5 70.6 %reduce-scatter.9.cloned.1.call-done = f32[6,4,8,128]{3,2,1,0:T(8,128)} async-done(((f32[6,4,128,128]{3,2,1,0:T(8,128)}), f32[6,4,8,128]{3,2,1,0:T(8,128)}) %reduce-scatter.9.cloned.1.call-update) | async-done | bytes 98320 | tf_op jit(solution)/shard_map/reduce_scatter | solution.py:129
  599.8 73.2 %psum.15 = f32[32,16,16]{2,1,0:T(8,128)S(1)} all-reduce(f32[32,16,16]{2,1,0:T(8,128)S(1)} %fusion.97), channel_id=1, replica_groups=mesh['seq'=16,'tp'=16] {'tp'}, use_global_device_ids=true, to_apply=%region_3.5 | all-reduce | flops 8192 | bytes 65536 | tf_op jit(solution)/shard_map/psum | solution.py:147
  674.9 80.0 %all-reduce.2.cloned.1.call-done = f32[1,512,512]{2,1,0:T(8,128)} async-done(((f32[1,512,512]{2,1,0:T(8,128)}), f32[1,512,512]{2,1,0:T(8,128)}) %all-reduce.2.cloned.1.call-update) | async-done | bytes 1048592 | tf_op jit(solution)/shard_map/psum | solution.py:147
  754.9 2.3 broadcast_multiply_fusion
  (178 shorter events, 63.7 us)
Async XLA Ops:
  7.2 16.0 %copy-start.37 = (bf16[32,16,16]{0,2,1:T(8,128)(2,1)S(1)}, bf16[32,16,16]{0,2,1:T(8,128)(2,1)}, u32[]{:S(2)}) copy-start(bf16[32,16,16]{0,2,1:T(8,128)(2,1)} %param.13) | copy-start | bytes 49156
  7.2 60.9 %all-gather.5.cloned.1.call-start = ((), (), s32[]{:S(2)}) async-start(), calls=%async_computation.10 | async-start | bytes 2228224 | tf_op jit(solution)/shard_map/all_gather | solution.py:69
  10.2 31.4 %copy-start.31 = (bf16[512,128]{1,0:T(8,128)(2,1)S(1)}, bf16[512,128]{1,0:T(8,128)(2,1)}, u32[]{:S(2)}) copy-start(bf16[512,128]{1,0:T(8,128)(2,1)} %param.11) | copy-start | bytes 393220
  12.3 30.1 %copy-start.38 = (s32[4,2]{0,1:T(2,128)S(1)}, s32[4,2]{0,1:T(2,128)}, u32[]{:S(2)}) copy-start(s32[4,2]{0,1:T(2,128)} %param.18) | copy-start | bytes 100
  13.0 17.6 %all-to-all-start = ((bf16[16,2,2048]{2,1,0:T(2,128)(2,1)}), bf16[16,2,2048]{2,1,0:T(2,128)(2,1)S(1)}, u32[]{:S(2)}, u32[]{:S(2)}) async-start(bf16[16,2,2048]{2,1,0:T(2,128)(2,1)} %reshape.151), calls=%async_computation | async-start | bytes 262144 | tf_op jit(solution)/shard_map/all_to_all | solution.py:55
  23.1 98.9 %all-gather.3.cloned.1.call-start = ((), (), s32[]{:S(2)}) async-start(), calls=%async_computation.8 | async-start | bytes 2228224 | tf_op jit(solution)/shard_map/all_gather | solution.py:68
  42.4 326.8 %reduce-scatter.7.cloned.1.call-start = ((), (), s32[]{:S(2)}) async-start(), calls=%async_computation.11 | async-start | bytes 4456448 | tf_op jit(solution)/shard_map/reduce_scatter | solution.py:126
  135.5 3.4 copy-start.21
  136.9 2.0 collective-permute-start
  139.2 13.6 %copy-start.9 = (bf16[512,4,128]{2,0,1:T(8,128)(2,1)}, bf16[512,4,128]{2,0,1:T(8,128)(2,1)S(1)}, u32[]{:S(2)}) copy-start(bf16[512,4,128]{2,0,1:T(8,128)(2,1)S(1)} %fusion.27) | copy-start | bytes 1572868
  139.3 13.3 %collective-permute-start.1 = (bf16[512,4,128]{2,0,1:T(8,128)(2,1)S(1)}, bf16[512,4,128]{2,0,1:T(8,128)(2,1)S(1)}, u32[]{:S(2)}, u32[]{:S(2)}) collective-permute-start(bf16[512,4,128]{2,0,1:T(8,128)(2,1)S(1)} %fusion.27), channel_id=1, source_target_pairs={{0,2},{1,3},{2,0},{3,1},{4,6},{5,7},{6,4},{7,5},{8,10},{9,11},{10,... | collective-permute-start | bytes 1572872 | tf_op jit(solution)/shard_map/ppermute | solution.py:11
  152.9 14.3 %copy-start.11 = (bf16[512,4,128]{2,0,1:T(8,128)(2,1)}, bf16[512,4,128]{2,0,1:T(8,128)(2,1)S(1)}, u32[]{:S(2)}) copy-start(bf16[512,4,128]{2,0,1:T(8,128)(2,1)S(1)} %fusion.26) | copy-start | bytes 1572868
  152.9 14.0 %collective-permute-start.2 = (bf16[512,4,128]{2,0,1:T(8,128)(2,1)S(1)}, bf16[512,4,128]{2,0,1:T(8,128)(2,1)S(1)}, u32[]{:S(2)}, u32[]{:S(2)}) collective-permute-start(bf16[512,4,128]{2,0,1:T(8,128)(2,1)S(1)} %fusion.26), channel_id=1, source_target_pairs={{0,4},{1,5},{2,6},{3,7},{4,0},{5,1},{6,2},{7,3},{8,12},{9,13},{10,... | collective-permute-start | bytes 1572872 | tf_op jit(solution)/shard_map/ppermute | solution.py:11
  167.1 13.4 %copy-start.13 = (bf16[512,4,128]{2,0,1:T(8,128)(2,1)}, bf16[512,4,128]{2,0,1:T(8,128)(2,1)S(1)}, u32[]{:S(2)}) copy-start(bf16[512,4,128]{2,0,1:T(8,128)(2,1)S(1)} %fusion.25) | copy-start | bytes 1572868
  167.2 13.1 %collective-permute-start.3 = (bf16[512,4,128]{2,0,1:T(8,128)(2,1)S(1)}, bf16[512,4,128]{2,0,1:T(8,128)(2,1)S(1)}, u32[]{:S(2)}, u32[]{:S(2)}) collective-permute-start(bf16[512,4,128]{2,0,1:T(8,128)(2,1)S(1)} %fusion.25), channel_id=1, source_target_pairs={{0,8},{1,9},{2,10},{3,11},{4,12},{5,13},{6,14},{7,15},{8,0},{9,1},... | collective-permute-start | bytes 1572872 | tf_op jit(solution)/shard_map/ppermute | solution.py:11
  167.8 12.8 %copy-start.33 = (bf16[8,512,128]{2,1,0:T(8,128)(2,1)S(1)}, bf16[8,512,128]{2,1,0:T(8,128)(2,1)}, u32[]{:S(2)}) copy-start(bf16[8,512,128]{2,1,0:T(8,128)(2,1)} %get-tuple-element.37) | copy-start | bytes 3145732
  167.8 12.8 %copy-start.36 = (bf16[4,2,128,128]{3,2,1,0:T(8,128)(2,1)S(1)}, bf16[4,2,128,128]{3,2,1,0:T(8,128)(2,1)}, u32[]{:S(2)}) copy-start(bf16[4,2,128,128]{3,2,1,0:T(8,128)(2,1)} %param.17) | copy-start | bytes 786436
  181.6 24.1 %copy-start.4 = (bf16[512,4,128]{2,0,1:T(8,128)(2,1)}, bf16[512,4,128]{2,0,1:T(8,128)(2,1)S(1)}, u32[]{:S(2)}) copy-start(bf16[512,4,128]{2,0,1:T(8,128)(2,1)S(1)} %fusion.52) | copy-start | bytes 1572868
  181.9 23.5 %collective-permute-start.4 = (f32[512,4,128]{2,0,1:T(8,128)S(1)}, f32[512,4,128]{2,0,1:T(8,128)S(1)}, u32[]{:S(2)}, u32[]{:S(2)}) collective-permute-start(f32[512,4,128]{2,0,1:T(8,128)S(1)} %convolution_bitcast_fusion.12), channel_id=1, source_target_pairs={{0,8},{1,9},{2,10},{3,11},{4,12},{5,13},{6,14},{7,15},{8,0},{9,1},... | collective-permute-start | bytes 3145736 | tf_op jit(solution)/shard_map/ppermute | solution.py:11
  206.0 22.8 %collective-permute-start.5 = (f32[512,4,128]{2,0,1:T(8,128)S(1)}, f32[512,4,128]{2,0,1:T(8,128)S(1)}, u32[]{:S(2)}, u32[]{:S(2)}) collective-permute-start(f32[512,4,128]{2,0,1:T(8,128)S(1)} %convolution_bitcast_fusion.10), channel_id=1, source_target_pairs={{0,4},{1,5},{2,6},{3,7},{4,0},{5,1},{6,2},{7,3},{8,12},{9,13},{10,... | collective-permute-start | bytes 3145736 | tf_op jit(solution)/shard_map/ppermute | solution.py:11
  229.4 19.7 %collective-permute-start.6 = (f32[512,4,128]{2,0,1:T(8,128)S(1)}, f32[512,4,128]{2,0,1:T(8,128)S(1)}, u32[]{:S(2)}, u32[]{:S(2)}) collective-permute-start(f32[512,4,128]{2,0,1:T(8,128)S(1)} %convolution_bitcast_fusion.8), channel_id=1, source_target_pairs={{0,2},{1,3},{2,0},{3,1},{4,6},{5,7},{6,4},{7,5},{8,10},{9,11},{10,... | collective-permute-start | bytes 3145736 | tf_op jit(solution)/shard_map/ppermute | solution.py:11
  249.8 8.3 %collective-permute-start.7 = (f32[512,4,128]{2,0,1:T(8,128)S(1)}, f32[512,4,128]{2,0,1:T(8,128)S(1)}, u32[]{:S(2)}, u32[]{:S(2)}) collective-permute-start(f32[512,4,128]{2,0,1:T(8,128)S(1)} %convolution_bitcast_fusion.6), channel_id=1, source_target_pairs={{0,1},{1,0},{2,3},{3,2},{4,5},{5,4},{6,7},{7,6},{8,9},{9,8},{10,11... | collective-permute-start | bytes 3145736 | tf_op jit(solution)/shard_map/ppermute | solution.py:11
  283.8 176.8 %reduce-scatter.5.cloned.1.call-start = ((), (), s32[]{:S(2)}) async-start(), calls=%async_computation.9 | async-start | bytes 4456448 | tf_op jit(solution)/shard_map/reduce_scatter | solution.py:99
  293.8 232.2 %reduce-scatter.11.cloned.1.call-start = ((), (), s32[]{:S(2)}) async-start(), calls=%async_computation.14 | async-start | bytes 1671168 | tf_op jit(solution)/shard_map/reduce_scatter | solution.py:130
  294.0 3.3 copy-start.23
  301.6 296.5 %reduce-scatter.9.cloned.1.call-start = ((), (), s32[]{:S(2)}) async-start(), calls=%async_computation.13 | async-start | bytes 1671168 | tf_op jit(solution)/shard_map/reduce_scatter | solution.py:129
  301.7 3.3 copy-start.8
  308.2 61.0 %copy-start.28 = (bf16[512,128]{0,1:T(8,128)(2,1)S(1)}, bf16[512,128]{0,1:T(8,128)(2,1)}, u32[]{:S(2)}) copy-start(bf16[512,128]{0,1:T(8,128)(2,1)} %copy.147) | copy-start | bytes 393220
  370.1 90.5 %copy-start.32 = (bf16[512,128]{1,0:T(8,128)(2,1)S(1)}, bf16[512,128]{1,0:T(8,128)(2,1)}, u32[]{:S(2)}) copy-start(bf16[512,128]{1,0:T(8,128)(2,1)} %fusion.65) | copy-start | bytes 393220
  386.9 75.3 %all-to-all-start.3 = ((bf16[16,32,128]{2,1,0:T(8,128)(2,1)}), bf16[16,32,128]{2,1,0:T(8,128)(2,1)S(1)}, u32[]{:S(2)}, u32[]{:S(2)}) async-start(bf16[16,32,128]{2,1,0:T(8,128)(2,1)} %copy.155), calls=%async_computation.5 | async-start | bytes 262144 | tf_op jit(solution)/shard_map/all_to_all | solution.py:142
  390.5 364.4 %all-reduce.2.cloned.1.call-start = ((), (), s32[]{:S(2)}) async-start(), calls=%async_computation.12 | async-start | bytes 2097152 | tf_op jit(solution)/shard_map/psum | solution.py:147
  463.5 210.3 %copy-start.35 = (f32[512,128]{0,1:T(8,128)S(1)}, f32[512,128]{0,1:T(8,128)}, u32[]{:S(2)}) copy-start(f32[512,128]{0,1:T(8,128)} %reduce-scatter.7.cloned.1.call-done) | copy-start | bytes 786436
  (24 other events, 46.9 us)
Sparse Core Ops, SparseCore 0:
  11.3 56.7 all-gather.4
  71.2 50.7 all-gather.2
  284.0 85.1 reduce-scatter.6
  373.3 87.2 reduce-scatter.4
  463.0 62.8 reduce-scatter.10
  528.4 69.6 reduce-scatter.8
  601.3 153.5 all-reduce.1
where the time goes:
time: 765 us; the launch traced here: 764 us
  waiting for transfers between devices  530 us (69%)
  blocking collectives  97.9 us (13%)
  matrix products  50.9 us (7%)
  local copies, waits for them, and re-layouts  33.1 us (4%)
  starting transfers between devices  24.3 us (3%)
  between operations  14.8 us (2%)
  other arithmetic  12.8 us (2%)
    ppermute x8, waiting for transfers between devices, partner_2(): return lax.ppermute(value, axis, pairs)  105 us
    psum x1, waiting for transfers between devices, per_device(): second_sum, first_sum = lax.psum((second_part, first_part), 'tp')  80 us
    psum x1, blocking collectives, per_device(): second_sum, first_sum = lax.psum((second_part, first_part), 'tp')  73.2 us
    reduce_scatter x1, waiting for transfers between devices, per_device(): lax.psum_scatter(jnp.stack(self_terms), 'seq', scatter_dimension=2, tiled...  70.6 us
    reduce_scatter x1, waiting for transfers between devices, per_device(): lax.psum_scatter(down_term, 'tp', scatter_dimension=1, tiled=True)  70.1 us
    reduce_scatter x1, waiting for transfers between devices, per_device(): lax.psum_scatter(jnp.stack(cross_terms), 'seq', scatter_dimension=2, tile...  62.4 us
    reduce_scatter x1, waiting for transfers between devices, per_device(): lax.psum_scatter(spread, 'tp', scatter_dimension=1, tiled=True)  59.9 us
    all_gather x1, waiting for transfers between devices, per_device(): lax.all_gather(hidden_in, 'tp', axis=1, tiled=True)  49.2 us
  transfers between devices with their start and end apart: 17, of which 16 were waited for; matrix products, arithmetic and copies ran while one was open for 6% of the time, Pallas kernels for 0%

commit v1 on v0

--- a/solution.py
+++ b/solution.py
@@ -64,8 +64,11 @@
     hidden_in = (
         tokens.astype(jnp.float32) + mixed_tokens.reshape(seq_len, width_local).astype(jnp.float32)
     ).astype(jnp.bfloat16)
+    _connect_page = lambda obj: jnp.concatenate(
+        lax.all_to_all(jnp.stack([obj for _ in range(lax.psum(1, "tp"))]), "tp", 0, 0), axis=1
+    )
     hidden_all, cotangent_all = (
-        lax.all_gather(hidden_in, "tp", axis=1, tiled=True),
+        _connect_page(hidden_in),
         lax.all_gather(cotangent, "tp", axis=1, tiled=True),
     )
     flat_pairs = block_pairs.reshape(-1)

time: 765 us -> 731 us (0.956)
  waiting for transfers between devices: 530 us -> 481 us
  starting transfers between devices: 24.3 us -> 41 us
    all_gather x1 -> x0, waiting for transfers between devices: 49.2 us -> none  [per_device(): lax.all_gather(hidden_in, 'tp', axis=1, tiled=True)]
    all_to_all x0 -> x1, waiting for transfers between devices: none -> 31.1 us  [per_device(): lax.all_to_all(jnp.stack([obj for _ in range(lax.psum(1, 'tp'))]), 'tp',...]
    all_gather x1, waiting for transfers between devices: 25.5 us -> 0.01 us  [per_device(): lax.all_gather(cotangent, 'tp', axis=1, tiled=True)]
    all_to_all x0 -> x1, starting transfers between devices: none -> 9.82 us  [per_device(): lax.all_to_all(jnp.stack([obj for _ in range(lax.psum(1, 'tp'))]), 'tp',...]
  transfers between devices with their start and end apart: 17 -> 17, of which waited for: 16 -> 15; matrix products, arithmetic and copies ran while one was open for 6% -> 6% of each run, Pallas kernels for 0% -> 0%
where the time goes in v1:
time: 731 us; the launch traced here: 730 us
  waiting for transfers between devices  481 us (66%)
  blocking collectives  98.2 us (13%)
  matrix products  50 us (7%)
  starting transfers between devices  41 us (6%)
  local copies, waits for them, and re-layouts  31.6 us (4%)
  between operations  14.8 us (2%)
  other arithmetic  13.7 us (2%)
    ppermute x8, waiting for transfers between devices, partner_2(): return lax.ppermute(value, axis, pairs)  101 us
    psum x1, waiting for transfers between devices, per_device(): second_sum, first_sum = lax.psum((second_part, first_part), 'tp')  79.7 us
    psum x1, blocking collectives, per_device(): second_sum, first_sum = lax.psum((second_part, first_part), 'tp')  73.5 us
    reduce_scatter x1, waiting for transfers between devices, per_device(): lax.psum_scatter(jnp.stack(self_terms), 'seq', scatter_dimension=2, tiled...  70.6 us
    reduce_scatter x1, waiting for transfers between devices, per_device(): lax.psum_scatter(down_term, 'tp', scatter_dimension=1, tiled=True)  70.3 us
    reduce_scatter x1, waiting for transfers between devices, per_device(): lax.psum_scatter(jnp.stack(cross_terms), 'seq', scatter_dimension=2, tile...  62.1 us
    reduce_scatter x1, waiting for transfers between devices, per_device(): lax.psum_scatter(spread, 'tp', scatter_dimension=1, tiled=True)  58.8 us
    all_to_all x1, waiting for transfers between devices, per_device(): lax.all_to_all(jnp.stack([obj for _ in range(lax.psum(1, 'tp'))]), 'tp',...  31.1 us
  transfers between devices with their start and end apart: 17, of which 15 were waited for; matrix products, arithmetic and copies ran while one was open for 6% of the time, Pallas kernels for 0%

profile of v1, /device:TPU:1, one launch (start us, length us, event | category | flops | bytes accessed | tf_op | source)
XLA Modules:
  0.0 730.2 jit_solution(15245738370927005198)
XLA Ops:
  13.0 10.0 %all-to-all-start = ((bf16[16,2,2048]{2,1,0:T(2,128)(2,1)}), bf16[16,2,2048]{2,1,0:T(2,128)(2,1)S(1)}, u32[]{:S(2)}, u32[]{:S(2)}) async-start(bf16[16,2,2048]{2,1,0:T(2,128)(2,1)} %reshape.153), calls=%async_computation | async-start | bytes 262144 | tf_op jit(solution)/shard_map/all_to_all | solution.py:55
  23.3 7.3 %all-to-all-done = bf16[16,2,2048]{2,1,0:T(2,128)(2,1)S(1)} async-done(((bf16[16,2,2048]{2,1,0:T(2,128)(2,1)}), bf16[16,2,2048]{2,1,0:T(2,128)(2,1)S(1)}, u32[]{:S(2)}, u32[]{:S(2)}) %all-to-all-start) | async-done | bytes 131104 | tf_op jit(solution)/shard_map/all_to_all | solution.py:55
  31.0 10.6 %all_to_all.47 = bf16[16,32,128]{2,1,0:T(8,128)(2,1)S(1)} all-to-all(bf16[16,32,128]{2,1,0:T(8,128)(2,1)S(1)} %copy.133), channel_id=1, replica_groups=mesh['seq'=16,'tp'=16] {'seq'}, dimensions={0} | all-to-all | bytes 262144 | tf_op jit(solution)/shard_map/all_to_all | solution.py:61
  43.5 9.8 %all-to-all-start.2 = ((bf16[16,512,128]{2,1,0:T(8,128)(2,1)}), bf16[16,512,128]{2,1,0:T(8,128)(2,1)S(1)}, u32[]{:S(2)}, u32[]{:S(2)}) async-start(bf16[16,512,128]{2,1,0:T(8,128)(2,1)} %stack.30), calls=%async_computation.2 | async-start | bytes 4194304 | tf_op jit(solution)/shard_map/all_to_all | solution.py:68
  53.6 31.1 %all-to-all-done.2 = bf16[16,512,128]{2,1,0:T(8,128)(2,1)S(1)} async-done(((bf16[16,512,128]{2,1,0:T(8,128)(2,1)}), bf16[16,512,128]{2,1,0:T(8,128)(2,1)S(1)}, u32[]{:S(2)}, u32[]{:S(2)}) %all-to-all-start.2) | async-done | bytes 2097184 | tf_op jit(solution)/shard_map/all_to_all | solution.py:68
  86.3 3.0 copy.142
  91.0 2.8 broadcast_select_fusion
  103.4 12.4 %collective-permute-done.1 = bf16[512,4,128]{2,0,1:T(8,128)(2,1)S(1)} collective-permute-done((bf16[512,4,128]{2,0,1:T(8,128)(2,1)S(1)}, bf16[512,4,128]{2,0,1:T(8,128)(2,1)S(1)}, u32[]{:S(2)}, u32[]{:S(2)}) %collective-permute-start.1) | collective-permute-done | bytes 524320 | tf_op jit(solution)/shard_map/ppermute | solution.py:11
  116.1 3.9 collective-permute-start.2
  120.2 11.1 %collective-permute-done.2 = bf16[512,4,128]{2,0,1:T(8,128)(2,1)S(1)} collective-permute-done((bf16[512,4,128]{2,0,1:T(8,128)(2,1)S(1)}, bf16[512,4,128]{2,0,1:T(8,128)(2,1)S(1)}, u32[]{:S(2)}, u32[]{:S(2)}) %collective-permute-start.2) | collective-permute-done | bytes 524320 | tf_op jit(solution)/shard_map/ppermute | solution.py:11
  134.7 10.9 %collective-permute-done.3 = bf16[512,4,128]{2,0,1:T(8,128)(2,1)S(1)} collective-permute-done((bf16[512,4,128]{2,0,1:T(8,128)(2,1)S(1)}, bf16[512,4,128]{2,0,1:T(8,128)(2,1)S(1)}, u32[]{:S(2)}, u32[]{:S(2)}) %collective-permute-start.3) | collective-permute-done | bytes 524320 | tf_op jit(solution)/shard_map/ppermute | solution.py:11
  147.5 2.4 collective-permute-start.4
  149.9 21.5 %collective-permute-done.4 = f32[512,4,128]{2,0,1:T(8,128)S(1)} collective-permute-done((f32[512,4,128]{2,0,1:T(8,128)S(1)}, f32[512,4,128]{2,0,1:T(8,128)S(1)}, u32[]{:S(2)}, u32[]{:S(2)}) %collective-permute-start.4) | collective-permute-done | bytes 1048608 | tf_op jit(solution)/shard_map/ppermute | solution.py:11
  172.1 2.4 collective-permute-start.5
  174.5 20.8 %collective-permute-done.5 = f32[512,4,128]{2,0,1:T(8,128)S(1)} collective-permute-done((f32[512,4,128]{2,0,1:T(8,128)S(1)}, f32[512,4,128]{2,0,1:T(8,128)S(1)}, u32[]{:S(2)}, u32[]{:S(2)}) %collective-permute-start.5) | collective-permute-done | bytes 1048608 | tf_op jit(solution)/shard_map/ppermute | solution.py:11
  196.0 20.6 %collective-permute-done.6 = f32[512,4,128]{2,0,1:T(8,128)S(1)} collective-permute-done((f32[512,4,128]{2,0,1:T(8,128)S(1)}, f32[512,4,128]{2,0,1:T(8,128)S(1)}, u32[]{:S(2)}, u32[]{:S(2)}) %collective-permute-start.6) | collective-permute-done | bytes 1048608 | tf_op jit(solution)/shard_map/ppermute | solution.py:11
  217.2 5.0 collective-permute-start.7
  226.1 2.3 rev.18
  234.5 3.2 convolution_bitcast_fusion.1
  237.8 7.2 convolution_bitcast_fusion
  245.0 5.4 copy.185
  253.0 4.1 fusion.1
  257.1 4.0 copy.203
  276.5 58.8 %reduce-scatter.7.cloned.1.call-done = f32[512,128]{0,1:T(8,128)} async-done(((f32[512,2048]{0,1:T(8,128)}), f32[512,128]{0,1:T(8,128)}) %reduce-scatter.7.cloned.1.call-update) | async-done | bytes 262160 | tf_op jit(solution)/shard_map/reduce_scatter | solution.py:129
  338.0 14.1 %all_to_all.48 = bf16[16,2,2048]{2,1,0:T(2,128)(2,1)S(1)} all-to-all(bf16[16,2,2048]{2,1,0:T(2,128)(2,1)S(1)} %reshape.155), channel_id=1, replica_groups=mesh['seq'=16,'tp'=16] {'seq'}, dimensions={0} | all-to-all | bytes 262144 | tf_op jit(solution)/shard_map/all_to_all | solution.py:135
  353.2 3.5 all-to-all-start.4
  356.7 70.3 %reduce-scatter.5.cloned.1.call-done = f32[512,128]{1,0:T(8,128)} async-done(((f32[512,2048]{1,0:T(8,128)}), f32[512,128]{1,0:T(8,128)}) %reduce-scatter.5.cloned.1.call-update) | async-done | bytes 262160 | tf_op jit(solution)/shard_map/reduce_scatter | solution.py:102
  429.9 62.1 %reduce-scatter.11.cloned.1.call-done = f32[6,4,8,128]{3,2,1,0:T(8,128)} async-done(((f32[6,4,128,128]{3,2,1,0:T(8,128)}), f32[6,4,8,128]{3,2,1,0:T(8,128)}) %reduce-scatter.11.cloned.1.call-update) | async-done | bytes 98320 | tf_op jit(solution)/shard_map/reduce_scatter | solution.py:133
  493.6 70.6 %reduce-scatter.9.cloned.1.call-done = f32[6,4,8,128]{3,2,1,0:T(8,128)} async-done(((f32[6,4,128,128]{3,2,1,0:T(8,128)}), f32[6,4,8,128]{3,2,1,0:T(8,128)}) %reduce-scatter.9.cloned.1.call-update) | async-done | bytes 98320 | tf_op jit(solution)/shard_map/reduce_scatter | solution.py:132
  565.9 73.5 %psum.15 = f32[32,16,16]{2,1,0:T(8,128)S(1)} all-reduce(f32[32,16,16]{2,1,0:T(8,128)S(1)} %fusion.97), channel_id=1, replica_groups=mesh['seq'=16,'tp'=16] {'tp'}, use_global_device_ids=true, to_apply=%region_3.5 | all-reduce | flops 8192 | bytes 65536 | tf_op jit(solution)/shard_map/psum | solution.py:150
  641.3 79.7 %all-reduce.2.cloned.1.call-done = f32[1,512,512]{2,1,0:T(8,128)} async-done(((f32[1,512,512]{2,1,0:T(8,128)}), f32[1,512,512]{2,1,0:T(8,128)}) %all-reduce.2.cloned.1.call-update) | async-done | bytes 1048592 | tf_op jit(solution)/shard_map/psum | solution.py:150
  721.0 2.3 broadcast_multiply_fusion
  (186 shorter events, 68.6 us)
Async XLA Ops:
  7.2 15.9 %copy-start.42 = (bf16[32,16,16]{0,2,1:T(8,128)(2,1)S(1)}, bf16[32,16,16]{0,2,1:T(8,128)(2,1)}, u32[]{:S(2)}) copy-start(bf16[32,16,16]{0,2,1:T(8,128)(2,1)} %param.13) | copy-start | bytes 49156
  7.2 79.1 %all-gather.2.cloned.1.call-start = ((), (), s32[]{:S(2)}) async-start(), calls=%async_computation.10 | async-start | bytes 2228224 | tf_op jit(solution)/shard_map/all_gather | solution.py:72
  10.2 31.4 %copy-start.30 = (bf16[512,128]{1,0:T(8,128)(2,1)S(1)}, bf16[512,128]{1,0:T(8,128)(2,1)}, u32[]{:S(2)}) copy-start(bf16[512,128]{1,0:T(8,128)(2,1)} %param.11) | copy-start | bytes 393220
  13.0 17.6 %all-to-all-start = ((bf16[16,2,2048]{2,1,0:T(2,128)(2,1)}), bf16[16,2,2048]{2,1,0:T(2,128)(2,1)S(1)}, u32[]{:S(2)}, u32[]{:S(2)}) async-start(bf16[16,2,2048]{2,1,0:T(2,128)(2,1)} %reshape.153), calls=%async_computation | async-start | bytes 262144 | tf_op jit(solution)/shard_map/all_to_all | solution.py:55
  30.8 12.7 %copy-start.32 = (bf16[1,512,128]{2,1,0:T(8,128)(2,1)}, bf16[1,512,128]{2,1,0:T(8,128)(2,1)S(1)}, u32[]{:S(2)}) copy-start(bf16[1,512,128]{2,1,0:T(8,128)(2,1)S(1)} %copy.186) | copy-start | bytes 393220
  43.5 9.9 %copy-start.43 = (s32[4,2]{0,1:T(2,128)S(1)}, s32[4,2]{0,1:T(2,128)}, u32[]{:S(2)}) copy-start(s32[4,2]{0,1:T(2,128)} %param.18) | copy-start | bytes 100
  43.5 41.2 %all-to-all-start.2 = ((bf16[16,512,128]{2,1,0:T(8,128)(2,1)}), bf16[16,512,128]{2,1,0:T(8,128)(2,1)S(1)}, u32[]{:S(2)}, u32[]{:S(2)}) async-start(bf16[16,512,128]{2,1,0:T(8,128)(2,1)} %stack.30), calls=%async_computation.2 | async-start | bytes 4194304 | tf_op jit(solution)/shard_map/all_to_all | solution.py:68
  53.3 282.0 %reduce-scatter.7.cloned.1.call-start = ((), (), s32[]{:S(2)}) async-start(), calls=%async_computation.11 | async-start | bytes 4456448 | tf_op jit(solution)/shard_map/reduce_scatter | solution.py:129
  99.6 2.2 collective-permute-start
  102.6 13.4 %copy-start.9 = (bf16[512,4,128]{2,0,1:T(8,128)(2,1)}, bf16[512,4,128]{2,0,1:T(8,128)(2,1)S(1)}, u32[]{:S(2)}) copy-start(bf16[512,4,128]{2,0,1:T(8,128)(2,1)S(1)} %fusion.27) | copy-start | bytes 1572868
  102.6 13.1 %collective-permute-start.1 = (bf16[512,4,128]{2,0,1:T(8,128)(2,1)S(1)}, bf16[512,4,128]{2,0,1:T(8,128)(2,1)S(1)}, u32[]{:S(2)}, u32[]{:S(2)}) collective-permute-start(bf16[512,4,128]{2,0,1:T(8,128)(2,1)S(1)} %fusion.27), channel_id=1, source_target_pairs={{0,2},{1,3},{2,0},{3,1},{4,6},{5,7},{6,4},{7,5},{8,10},{9,11},{10,... | collective-permute-start | bytes 1572872 | tf_op jit(solution)/shard_map/ppermute | solution.py:11
  116.0 15.5 %copy-start.11 = (bf16[512,4,128]{2,0,1:T(8,128)(2,1)}, bf16[512,4,128]{2,0,1:T(8,128)(2,1)S(1)}, u32[]{:S(2)}) copy-start(bf16[512,4,128]{2,0,1:T(8,128)(2,1)S(1)} %fusion.26) | copy-start | bytes 1572868
  116.1 15.2 %collective-permute-start.2 = (bf16[512,4,128]{2,0,1:T(8,128)(2,1)S(1)}, bf16[512,4,128]{2,0,1:T(8,128)(2,1)S(1)}, u32[]{:S(2)}, u32[]{:S(2)}) collective-permute-start(bf16[512,4,128]{2,0,1:T(8,128)(2,1)S(1)} %fusion.26), channel_id=1, source_target_pairs={{0,4},{1,5},{2,6},{3,7},{4,0},{5,1},{6,2},{7,3},{8,12},{9,13},{10,... | collective-permute-start | bytes 1572872 | tf_op jit(solution)/shard_map/ppermute | solution.py:11
  132.1 13.8 %copy-start.13 = (bf16[512,4,128]{2,0,1:T(8,128)(2,1)}, bf16[512,4,128]{2,0,1:T(8,128)(2,1)S(1)}, u32[]{:S(2)}) copy-start(bf16[512,4,128]{2,0,1:T(8,128)(2,1)S(1)} %fusion.25) | copy-start | bytes 1572868
  132.1 13.5 %collective-permute-start.3 = (bf16[512,4,128]{2,0,1:T(8,128)(2,1)S(1)}, bf16[512,4,128]{2,0,1:T(8,128)(2,1)S(1)}, u32[]{:S(2)}, u32[]{:S(2)}) collective-permute-start(bf16[512,4,128]{2,0,1:T(8,128)(2,1)S(1)} %fusion.25), channel_id=1, source_target_pairs={{0,8},{1,9},{2,10},{3,11},{4,12},{5,13},{6,14},{7,15},{8,0},{9,1},... | collective-permute-start | bytes 1572872 | tf_op jit(solution)/shard_map/ppermute | solution.py:11
  134.7 11.7 %copy-start.36 = (bf16[8,512,128]{2,1,0:T(8,128)(2,1)S(1)}, bf16[8,512,128]{2,1,0:T(8,128)(2,1)}, u32[]{:S(2)}) copy-start(bf16[8,512,128]{2,1,0:T(8,128)(2,1)} %get-tuple-element.37) | copy-start | bytes 3145732
  134.7 11.7 %copy-start.40 = (bf16[4,2,128,128]{3,2,1,0:T(8,128)(2,1)S(1)}, bf16[4,2,128,128]{3,2,1,0:T(8,128)(2,1)}, u32[]{:S(2)}) copy-start(bf16[4,2,128,128]{3,2,1,0:T(8,128)(2,1)} %param.17) | copy-start | bytes 786436
  147.2 24.5 %copy-start.4 = (bf16[512,4,128]{2,0,1:T(8,128)(2,1)}, bf16[512,4,128]{2,0,1:T(8,128)(2,1)S(1)}, u32[]{:S(2)}) copy-start(bf16[512,4,128]{2,0,1:T(8,128)(2,1)S(1)} %fusion.52) | copy-start | bytes 1572868
  147.5 23.9 %collective-permute-start.4 = (f32[512,4,128]{2,0,1:T(8,128)S(1)}, f32[512,4,128]{2,0,1:T(8,128)S(1)}, u32[]{:S(2)}, u32[]{:S(2)}) collective-permute-start(f32[512,4,128]{2,0,1:T(8,128)S(1)} %convolution_bitcast_fusion.12), channel_id=1, source_target_pairs={{0,8},{1,9},{2,10},{3,11},{4,12},{5,13},{6,14},{7,15},{8,0},{9,1},... | collective-permute-start | bytes 3145736 | tf_op jit(solution)/shard_map/ppermute | solution.py:11
  172.1 23.2 %collective-permute-start.5 = (f32[512,4,128]{2,0,1:T(8,128)S(1)}, f32[512,4,128]{2,0,1:T(8,128)S(1)}, u32[]{:S(2)}, u32[]{:S(2)}) collective-permute-start(f32[512,4,128]{2,0,1:T(8,128)S(1)} %convolution_bitcast_fusion.10), channel_id=1, source_target_pairs={{0,4},{1,5},{2,6},{3,7},{4,0},{5,1},{6,2},{7,3},{8,12},{9,13},{10,... | collective-permute-start | bytes 3145736 | tf_op jit(solution)/shard_map/ppermute | solution.py:11
  195.9 20.7 %collective-permute-start.6 = (f32[512,4,128]{2,0,1:T(8,128)S(1)}, f32[512,4,128]{2,0,1:T(8,128)S(1)}, u32[]{:S(2)}, u32[]{:S(2)}) collective-permute-start(f32[512,4,128]{2,0,1:T(8,128)S(1)} %convolution_bitcast_fusion.8), channel_id=1, source_target_pairs={{0,2},{1,3},{2,0},{3,1},{4,6},{5,7},{6,4},{7,5},{8,10},{9,11},{10,... | collective-permute-start | bytes 3145736 | tf_op jit(solution)/shard_map/ppermute | solution.py:11
  217.2 7.3 %collective-permute-start.7 = (f32[512,4,128]{2,0,1:T(8,128)S(1)}, f32[512,4,128]{2,0,1:T(8,128)S(1)}, u32[]{:S(2)}, u32[]{:S(2)}) collective-permute-start(f32[512,4,128]{2,0,1:T(8,128)S(1)} %convolution_bitcast_fusion.6), channel_id=1, source_target_pairs={{0,1},{1,0},{2,3},{3,2},{4,5},{5,4},{6,7},{7,6},{8,9},{9,8},{10,11... | collective-permute-start | bytes 3145736 | tf_op jit(solution)/shard_map/ppermute | solution.py:11
  250.4 176.6 %reduce-scatter.5.cloned.1.call-start = ((), (), s32[]{:S(2)}) async-start(), calls=%async_computation.9 | async-start | bytes 4456448 | tf_op jit(solution)/shard_map/reduce_scatter | solution.py:102
  261.1 230.9 %reduce-scatter.11.cloned.1.call-start = ((), (), s32[]{:S(2)}) async-start(), calls=%async_computation.14 | async-start | bytes 1671168 | tf_op jit(solution)/shard_map/reduce_scatter | solution.py:133
  268.9 295.3 %reduce-scatter.9.cloned.1.call-start = ((), (), s32[]{:S(2)}) async-start(), calls=%async_computation.13 | async-start | bytes 1671168 | tf_op jit(solution)/shard_map/reduce_scatter | solution.py:132
  275.4 59.9 %copy-start.27 = (bf16[512,128]{0,1:T(8,128)(2,1)S(1)}, bf16[512,128]{0,1:T(8,128)(2,1)}, u32[]{:S(2)}) copy-start(bf16[512,128]{0,1:T(8,128)(2,1)} %copy.140) | copy-start | bytes 393220
  336.3 90.7 %copy-start.35 = (bf16[512,128]{1,0:T(8,128)(2,1)S(1)}, bf16[512,128]{1,0:T(8,128)(2,1)}, u32[]{:S(2)}) copy-start(bf16[512,128]{1,0:T(8,128)(2,1)} %copy-done.34) | copy-start | bytes 393220
  336.5 92.1 %copy-start.31 = (bf16[512,128]{1,0:T(8,128)(2,1)S(1)}, bf16[512,128]{1,0:T(8,128)(2,1)}, u32[]{:S(2)}) copy-start(bf16[512,128]{1,0:T(8,128)(2,1)} %param.11) | copy-start | bytes 393220
  353.2 75.5 %all-to-all-start.4 = ((bf16[16,32,128]{2,1,0:T(8,128)(2,1)}), bf16[16,32,128]{2,1,0:T(8,128)(2,1)S(1)}, u32[]{:S(2)}, u32[]{:S(2)}) async-start(bf16[16,32,128]{2,1,0:T(8,128)(2,1)} %copy.148), calls=%async_computation.6 | async-start | bytes 262144 | tf_op jit(solution)/shard_map/all_to_all | solution.py:145
  356.7 209.0 %copy-start.33 = (bf16[1,512,128]{2,1,0:T(8,128)(2,1)S(1)}, bf16[1,512,128]{2,1,0:T(8,128)(2,1)}, u32[]{:S(2)}) copy-start(bf16[1,512,128]{2,1,0:T(8,128)(2,1)} %copy-done.32) | copy-start | bytes 393220
  356.7 364.3 %all-reduce.2.cloned.1.call-start = ((), (), s32[]{:S(2)}) async-start(), calls=%async_computation.12 | async-start | bytes 2097152 | tf_op jit(solution)/shard_map/psum | solution.py:150
  429.9 210.4 %copy-start.39 = (f32[512,128]{0,1:T(8,128)S(1)}, f32[512,128]{0,1:T(8,128)}, u32[]{:S(2)}) copy-start(f32[512,128]{0,1:T(8,128)} %reduce-scatter.7.cloned.1.call-done) | copy-start | bytes 786436
  (29 other events, 65.4 us)
Sparse Core Ops, SparseCore 0:
  11.3 68.7 all-gather.1
  250.5 84.8 reduce-scatter.6
  339.6 87.3 reduce-scatter.4
  429.4 62.5 reduce-scatter.10
  494.4 69.7 reduce-scatter.8
  567.2 153.7 all-reduce.1
